TPU v7x, 256 devices: a whole 4x4x8 slice. The times are simulated.
256 devices in a mesh: rows: 256 (over z, x, y, core).
Axes of the slice: x: 4, y: 4, z: 8, core: 2. Of those that a mesh axis runs over, the one named last changes fastest.
Arguments:
- matrix: float32 [1048576, 128], P('rows')
- flips: int32 [1048576], P('rows'), may hold values from 0 to 1
- picks: int32 [16384], P('rows'), may hold values from 0 to 4095, as said below
Outputs:
- sketch: float32 [16384, 128], P('rows')
- factor: float32 [128, 128], replicated
Inputs may be any that keep to these rules, and one draw needn't show every extreme that they name: `picks`: each index lies within its owner's slab; repeated indices may occur.
All inputs are finite; a program needn't handle non-finite values.
Results may differ from a plain program's by a relative error of at most 0.00014.
Values sent between devices are 32-bit elements; how exact they have to be, the bound alone decides.
A program may use at most 64 MiB of HBM per device.

v0:
```python
import math
import jax
import jax.numpy as jnp
from jax import lax
from jax.sharding import PartitionSpec as P


def swapped(value, axis, stride):
    mask = 2**stride
    pairs = [(source, source ^ mask) for source in range(lax.axis_size(axis))]
    return lax.ppermute(value, axis, pairs)


def hadamard(order):
    index = lax.iota(jnp.int32, order)
    parity_sum = jnp.zeros((order, order), jnp.int32)
    for digit in range(order.bit_length()):
        parity_sum = parity_sum + (index[:, None] >> digit & 1) * (index[None, :] >> digit & 1)
    return (1 - 2 * (parity_sum % 2)).astype(jnp.float32)


def slab_transform(values):
    height = values.shape[0]
    width = values.shape[1]
    inner = 128
    outer = height // inner
    blocks = values.reshape(outer, inner, width)
    mixed = jnp.einsum(
        "ij,ajc->aic",
        hadamard(inner),
        blocks,
        precision=lax.Precision.HIGHEST,
        preferred_element_type=jnp.float32,
    )
    mixed = jnp.einsum(
        "ab,bic->aic",
        hadamard(outer),
        mixed,
        precision=lax.Precision.HIGHEST,
        preferred_element_type=jnp.float32,
    )
    return mixed.reshape(height, width)


def shards(matrix, flips, picks):
    devices = lax.axis_size("rows")
    digits = devices.bit_length() - 1
    myself = lax.axis_index("rows")
    height = matrix.shape[0]
    per_device = picks.shape[0]
    signs = (1 - 2 * flips).astype(jnp.float32)
    local = slab_transform(matrix * signs[:, None])
    scale = 1.0 / math.sqrt(height * devices)
    order_list = list(range(digits))
    values = local
    for digit in order_list:
        partner = swapped(values, "rows", digit)
        upper = myself >> digit & 1 == 1
        values = jnp.where(upper, partner - values, values + partner)
    sketch = jnp.take(values, picks, axis=0) * scale
    partial_gram = jnp.dot(
        sketch.T, sketch, preferred_element_type=jnp.float32, precision=lax.Precision.HIGHEST
    )
    gram = lax.psum(partial_gram, "rows") / (per_device * devices)
    factor = jnp.linalg.cholesky(gram)
    return (sketch, factor)


def solution(mesh):
    placed = (P("rows", None), P("rows"), P("rows"))
    return jax.shard_map(
        shards, mesh=mesh, in_specs=placed, out_specs=(P("rows", None), P()), check_vma=False
    )
```

profile of v0, /device:TPU:1, one launch (start us, length us, event | category | flops | bytes accessed | tf_op | source)
XLA Modules:
  0.0 735.6 jit_solution(15239661016108178442)
XLA Ops:
  8.0 2.2 broadcast_multiply_fusion
  10.2 5.0 fusion.7
  15.2 2.4 copy.10
  17.6 1.9 fusion
  19.5 1.2 copy.7
  20.7 3.3 collective-permute-start
  24.0 3.9 collective-permute-done
  28.0 2.4 add_select_fusion.7
  30.5 1.2 copy-done.1
  31.7 45.7 %collective-permute-done.1 = f32[4096,128]{1,0:T(8,128)} collective-permute-done((f32[4096,128]{1,0:T(8,128)S(1)}, f32[4096,128]{1,0:T(8,128)}, u32[]{:S(2)}, u32[]{:S(2)}) %collective-permute-start.1) | collective-permute-done | bytes 2097184 | tf_op jit(solution)/shard_map/ppermute | solution.py:11
  77.4 2.4 add_select_fusion.6
  79.9 1.3 collective-permute-start.2
  81.2 46.4 %collective-permute-done.2 = f32[4096,128]{1,0:T(8,128)} collective-permute-done((f32[4096,128]{1,0:T(8,128)S(1)}, f32[4096,128]{1,0:T(8,128)}, u32[]{:S(2)}, u32[]{:S(2)}) %collective-permute-start.2) | collective-permute-done | bytes 2097184 | tf_op jit(solution)/shard_map/ppermute | solution.py:11
  127.5 3.1 add_select_fusion.5
  130.7 45.4 %collective-permute-done.3 = f32[4096,128]{1,0:T(8,128)} collective-permute-done((f32[4096,128]{1,0:T(8,128)}, f32[4096,128]{1,0:T(8,128)}, u32[]{:S(2)}, u32[]{:S(2)}) %collective-permute-start.3) | collective-permute-done | bytes 2097184 | tf_op jit(solution)/shard_map/ppermute | solution.py:11
  176.1 2.4 add_select_fusion.4
  178.5 1.1 collective-permute-start.4
  179.7 44.8 %collective-permute-done.4 = f32[4096,128]{1,0:T(8,128)} collective-permute-done((f32[4096,128]{1,0:T(8,128)S(1)}, f32[4096,128]{1,0:T(8,128)}, u32[]{:S(2)}, u32[]{:S(2)}) %collective-permute-start.4) | collective-permute-done | bytes 2097184 | tf_op jit(solution)/shard_map/ppermute | solution.py:11
  224.5 3.1 add_select_fusion.3
  227.6 43.7 %collective-permute-done.5 = f32[4096,128]{1,0:T(8,128)} collective-permute-done((f32[4096,128]{1,0:T(8,128)}, f32[4096,128]{1,0:T(8,128)}, u32[]{:S(2)}, u32[]{:S(2)}) %collective-permute-start.5) | collective-permute-done | bytes 2097184 | tf_op jit(solution)/shard_map/ppermute | solution.py:11
  271.3 2.4 add_select_fusion.2
  273.8 1.7 collective-permute-start.6
  275.5 91.6 %collective-permute-done.6 = f32[4096,128]{1,0:T(8,128)} collective-permute-done((f32[4096,128]{1,0:T(8,128)S(1)}, f32[4096,128]{1,0:T(8,128)}, u32[]{:S(2)}, u32[]{:S(2)}) %collective-permute-start.6) | collective-permute-done | bytes 2097184 | tf_op jit(solution)/shard_map/ppermute | solution.py:11
  367.1 2.4 add_select_fusion.1
  369.5 5.1 collective-permute-start.7
  374.7 90.6 %collective-permute-done.7 = f32[4096,128]{1,0:T(8,128)} collective-permute-done((f32[4096,128]{1,0:T(8,128)S(1)}, f32[4096,128]{1,0:T(8,128)}, u32[]{:S(2)}, u32[]{:S(2)}) %collective-permute-start.7) | collective-permute-done | bytes 2097184 | tf_op jit(solution)/shard_map/ppermute | solution.py:11
  465.3 3.1 add_select_fusion
  468.4 2.2 gather_fusion
  470.7 0.9 fusion.62
  471.7 241.6 %all-reduce.2.cloned.1.call-done = f32[128,128]{0,1:T(8,128)} async-done(((f32[128,128]{0,1:T(8,128)}), f32[128,128]{0,1:T(8,128)}) %all-reduce.2.cloned.1.call-update) | async-done | bytes 65552 | tf_op jit(solution)/shard_map/psum | solution.py:64
  715.0 11.7 %cholesky.18 = f32[128,128]{1,0:T(8,128)S(1)} custom-call(f32[128,128]{1,0:T(8,128)S(1)} %fusion.9), custom_call_target="Cholesky" | custom-call | tf_op jit(solution)/shard_map/jit(cholesky)/cholesky | solution.py:65
  727.4 1.3 select_select_fusion
  (31 shorter events, 3.5 us)
Async XLA Ops:
  7.2 706.1 %all-reduce.2.cloned.1.call-start = ((), (), s32[]{:S(2)}) async-start(), calls=%async_computation | async-start | bytes 131072 | tf_op jit(solution)/shard_map/psum | solution.py:64
  20.7 3.3 copy-start.2
  20.7 7.2 collective-permute-start
  30.4 1.3 copy-start.1
  30.4 47.0 %collective-permute-start.1 = (f32[4096,128]{1,0:T(8,128)S(1)}, f32[4096,128]{1,0:T(8,128)}, u32[]{:S(2)}, u32[]{:S(2)}) collective-permute-start(f32[4096,128]{1,0:T(8,128)S(1)} %add_select_fusion.7), channel_id=1, source_target_pairs={{0,2},{1,3},{2,0},{3,1},{4,6},{5,7},{6,4},{7,5},{8,10},{9,11},{10,... | collective-permute-start | bytes 6291464 | tf_op jit(solution)/shard_map/ppermute | solution.py:11
  79.9 47.7 %collective-permute-start.2 = (f32[4096,128]{1,0:T(8,128)S(1)}, f32[4096,128]{1,0:T(8,128)}, u32[]{:S(2)}, u32[]{:S(2)}) collective-permute-start(f32[4096,128]{1,0:T(8,128)S(1)} %add_select_fusion.6), channel_id=1, source_target_pairs={{0,4},{1,5},{2,6},{3,7},{4,0},{5,1},{6,2},{7,3},{8,12},{9,13},{10,... | collective-permute-start | bytes 6291464 | tf_op jit(solution)/shard_map/ppermute | solution.py:11
  130.7 45.4 %collective-permute-start.3 = (f32[4096,128]{1,0:T(8,128)}, f32[4096,128]{1,0:T(8,128)}, u32[]{:S(2)}, u32[]{:S(2)}) collective-permute-start(f32[4096,128]{1,0:T(8,128)} %add_select_fusion.5), channel_id=1, source_target_pairs={{0,8},{1,9},{2,10},{3,11},{4,12},{5,13},{6,14},{7,15},{8,0},{9,1},... | collective-permute-start | bytes 6291464 | tf_op jit(solution)/shard_map/ppermute | solution.py:11
  178.5 45.9 %collective-permute-start.4 = (f32[4096,128]{1,0:T(8,128)S(1)}, f32[4096,128]{1,0:T(8,128)}, u32[]{:S(2)}, u32[]{:S(2)}) collective-permute-start(f32[4096,128]{1,0:T(8,128)S(1)} %add_select_fusion.4), channel_id=1, source_target_pairs={{0,16},{1,17},{2,18},{3,19},{4,20},{5,21},{6,22},{7,23},{8,24},{9,... | collective-permute-start | bytes 6291464 | tf_op jit(solution)/shard_map/ppermute | solution.py:11
  227.6 43.7 %collective-permute-start.5 = (f32[4096,128]{1,0:T(8,128)}, f32[4096,128]{1,0:T(8,128)}, u32[]{:S(2)}, u32[]{:S(2)}) collective-permute-start(f32[4096,128]{1,0:T(8,128)} %add_select_fusion.3), channel_id=1, source_target_pairs={{0,32},{1,33},{2,34},{3,35},{4,36},{5,37},{6,38},{7,39},{8,40},{9,... | collective-permute-start | bytes 6291464 | tf_op jit(solution)/shard_map/ppermute | solution.py:11
  273.8 1.7 copy-start
  273.8 93.3 %collective-permute-start.6 = (f32[4096,128]{1,0:T(8,128)S(1)}, f32[4096,128]{1,0:T(8,128)}, u32[]{:S(2)}, u32[]{:S(2)}) collective-permute-start(f32[4096,128]{1,0:T(8,128)S(1)} %add_select_fusion.2), channel_id=1, source_target_pairs={{0,64},{1,65},{2,66},{3,67},{4,68},{5,69},{6,70},{7,71},{8,72},{9,... | collective-permute-start | bytes 6291464 | tf_op jit(solution)/shard_map/ppermute | solution.py:11
  275.5 99.2 %copy-start.4 = (s32[64]{0:T(128)S(1)}, s32[64]{0:T(128)}, u32[]{:S(2)}) copy-start(s32[64]{0:T(128)} %param.5) | copy-start | bytes 772
  369.5 95.8 %collective-permute-start.7 = (f32[4096,128]{1,0:T(8,128)S(1)}, f32[4096,128]{1,0:T(8,128)}, u32[]{:S(2)}, u32[]{:S(2)}) collective-permute-start(f32[4096,128]{1,0:T(8,128)S(1)} %add_select_fusion.1), channel_id=1, source_target_pairs={{0,128},{1,129},{2,130},{3,131},{4,132},{5,133},{6,134},{7,135},{8... | collective-permute-start | bytes 6291464 | tf_op jit(solution)/shard_map/ppermute | solution.py:11
  470.7 258.0 %copy-start.3 = (f32[64,128]{1,0:T(8,128)}, f32[64,128]{1,0:T(8,128)S(1)}, u32[]{:S(2)}) copy-start(f32[64,128]{1,0:T(8,128)S(1)} %select_multiply_fusion) | copy-start | bytes 98308
Sparse Core Ops, SparseCore 0:
  471.8 241.3 all-reduce.1
where the time goes:
time: 736 us
  waiting for transfers between devices  654 us (89%)
  other arithmetic  40.1 us (5%)
  between operations  14.2 us (2%)
  starting transfers between devices  12.7 us (2%)
  matrix products  7.84 us (1%)
    ppermute x8, waiting for transfers between devices, swapped(): return lax.ppermute(value, axis, pairs)  412 us
    psum x1, waiting for transfers between devices, shards(): gram = lax.psum(partial_gram, 'rows') / (per_device * devices)  242 us
    select_n x8, other arithmetic, shards(): values = jnp.where(upper, partner - values, values + partner)  21.6 us
  transfers between devices with their start and end apart: 9, of which 9 were waited for; matrix products, arithmetic and copies ran while one was open for 0% of the time, Pallas kernels for 0%

commit v1 on v0

--- a/solution.py
+++ b/solution.py
@@ -61,7 +61,7 @@
     partial_gram = jnp.dot(
         sketch.T, sketch, preferred_element_type=jnp.float32, precision=lax.Precision.HIGHEST
     )
-    gram = lax.psum(partial_gram, "rows") / (per_device * devices)
+    gram = jnp.sum(lax.all_gather(partial_gram, "rows"), axis=0) / (per_device * devices)
     factor = jnp.linalg.cholesky(gram)
     return (sketch, factor)
 

time: 736 us -> 625 us (0.85)
  waiting for transfers between devices: 654 us -> 538 us
    psum x1 -> x0, waiting for transfers between devices: 242 us -> none  [shards(): gram = lax.psum(partial_gram, 'rows') / (per_device * devices)]
    all_gather x0 -> x1, waiting for transfers between devices: none -> 125 us  [shards(): lax.all_gather(partial_gram, 'rows')]
where the time goes in v1:
time: 625 us; the launch traced here: 624 us
  waiting for transfers between devices  538 us (86%)
  other arithmetic  45 us (7%)
  between operations  14.2 us (2%)
  starting transfers between devices  12.7 us (2%)
  matrix products  7.83 us (1%)
  local copies, waits for them, and re-layouts  7.11 us (1%)
    ppermute x8, waiting for transfers between devices, swapped(): return lax.ppermute(value, axis, pairs)  412 us
    all_gather x1, waiting for transfers between devices, shards(): lax.all_gather(partial_gram, 'rows')  125 us
    select_n x8, other arithmetic, shards(): values = jnp.where(upper, partner - values, values + partner)  21.6 us
    ppermute x8, starting transfers between devices, swapped(): return lax.ppermute(value, axis, pairs)  12.6 us
  transfers between devices with their start and end apart: 9, of which 9 were waited for; matrix products, arithmetic and copies ran while one was open for 0% of the time, Pallas kernels for 0%

profile of v1, /device:TPU:1, one launch (start us, length us, event | category | flops | bytes accessed | tf_op | source)
XLA Modules:
  0.0 624.4 jit_solution(3989698631527770779)
XLA Ops:
  8.0 2.2 broadcast_multiply_fusion
  10.2 5.0 convolution_bitcast_fusion
  15.2 2.4 copy.9
  17.6 1.9 fusion.34
  19.5 1.2 copy.10
  20.7 3.3 collective-permute-start
  24.0 3.9 collective-permute-done
  28.0 2.4 add_select_fusion.7
  30.5 1.2 copy-done.1
  31.7 45.7 %collective-permute-done.1 = f32[4096,128]{1,0:T(8,128)} collective-permute-done((f32[4096,128]{1,0:T(8,128)S(1)}, f32[4096,128]{1,0:T(8,128)}, u32[]{:S(2)}, u32[]{:S(2)}) %collective-permute-start.1) | collective-permute-done | bytes 2097184 | tf_op jit(solution)/shard_map/ppermute | solution.py:11
  77.4 2.4 add_select_fusion.6
  79.9 1.3 collective-permute-start.2
  81.2 46.4 %collective-permute-done.2 = f32[4096,128]{1,0:T(8,128)} collective-permute-done((f32[4096,128]{1,0:T(8,128)S(1)}, f32[4096,128]{1,0:T(8,128)}, u32[]{:S(2)}, u32[]{:S(2)}) %collective-permute-start.2) | collective-permute-done | bytes 2097184 | tf_op jit(solution)/shard_map/ppermute | solution.py:11
  127.5 3.1 add_select_fusion.5
  130.7 45.4 %collective-permute-done.3 = f32[4096,128]{1,0:T(8,128)} collective-permute-done((f32[4096,128]{1,0:T(8,128)}, f32[4096,128]{1,0:T(8,128)}, u32[]{:S(2)}, u32[]{:S(2)}) %collective-permute-start.3) | collective-permute-done | bytes 2097184 | tf_op jit(solution)/shard_map/ppermute | solution.py:11
  176.1 2.4 add_select_fusion.4
  178.5 1.1 collective-permute-start.4
  179.7 44.8 %collective-permute-done.4 = f32[4096,128]{1,0:T(8,128)} collective-permute-done((f32[4096,128]{1,0:T(8,128)S(1)}, f32[4096,128]{1,0:T(8,128)}, u32[]{:S(2)}, u32[]{:S(2)}) %collective-permute-start.4) | collective-permute-done | bytes 2097184 | tf_op jit(solution)/shard_map/ppermute | solution.py:11
  224.5 3.1 add_select_fusion.3
  227.6 43.7 %collective-permute-done.5 = f32[4096,128]{1,0:T(8,128)} collective-permute-done((f32[4096,128]{1,0:T(8,128)}, f32[4096,128]{1,0:T(8,128)}, u32[]{:S(2)}, u32[]{:S(2)}) %collective-permute-start.5) | collective-permute-done | bytes 2097184 | tf_op jit(solution)/shard_map/ppermute | solution.py:11
  271.3 2.4 add_select_fusion.2
  273.8 1.7 collective-permute-start.6
  275.5 91.6 %collective-permute-done.6 = f32[4096,128]{1,0:T(8,128)} collective-permute-done((f32[4096,128]{1,0:T(8,128)S(1)}, f32[4096,128]{1,0:T(8,128)}, u32[]{:S(2)}, u32[]{:S(2)}) %collective-permute-start.6) | collective-permute-done | bytes 2097184 | tf_op jit(solution)/shard_map/ppermute | solution.py:11
  367.1 2.4 add_select_fusion.1
  369.5 5.1 collective-permute-start.7
  374.7 90.6 %collective-permute-done.7 = f32[4096,128]{1,0:T(8,128)} collective-permute-done((f32[4096,128]{1,0:T(8,128)S(1)}, f32[4096,128]{1,0:T(8,128)}, u32[]{:S(2)}, u32[]{:S(2)}) %collective-permute-start.7) | collective-permute-done | bytes 2097184 | tf_op jit(solution)/shard_map/ppermute | solution.py:11
  465.3 3.1 add_select_fusion
  468.4 2.2 gather_fusion
  471.7 125.5 %all-gather.3.cloned.1.call-done = f32[32768,128]{1,0:T(8,128)} async-done(((f32[128,128]{1,0:T(8,128)}), f32[32768,128]{1,0:T(8,128)}) %all-gather.3.cloned.1.call-update) | async-done | bytes 16777232 | tf_op jit(solution)/shard_map/all_gather | solution.py:64
  597.1 6.6 %reduce_sum.11 = f32[128,128]{1,0:T(8,128)S(1)} reduce(f32[256,128,128]{2,1,0:T(8,128)} %bitcast.20, f32[]{:T(128)} %constant.127.clone.1), dimensions={0}, to_apply=%region_0.1 | reduce | flops 4177920 | bytes 16842756 | tf_op jit(solution)/shard_map/reduce_sum | solution.py:64
  603.8 11.7 %cholesky.18 = f32[128,128]{1,0:T(8,128)S(1)} custom-call(f32[128,128]{1,0:T(8,128)S(1)} %fusion.6), custom_call_target="Cholesky" | custom-call | tf_op jit(solution)/shard_map/jit(cholesky)/cholesky | solution.py:65
  616.3 1.3 select_select_fusion
  (31 shorter events, 2.8 us)
Async XLA Ops:
  7.2 590.0 %all-gather.3.cloned.1.call-start = ((), (), s32[]{:S(2)}) async-start(), calls=%async_computation | async-start | bytes 16842752 | tf_op jit(solution)/shard_map/all_gather | solution.py:64
  20.7 3.3 copy-start.2
  20.7 7.2 %collective-permute-start = (f32[4096,128]{1,0:T(8,128)S(1)}, f32[4096,128]{1,0:T(8,128)}, u32[]{:S(2)}, u32[]{:S(2)}) collective-permute-start(f32[4096,128]{1,0:T(8,128)S(1)} %bitcast.21), channel_id=1, source_target_pairs={{0,1},{1,0},{2,3},{3,2},{4,5},{5,4},{6,7},{7,6},{8,9},{9,8},{10,11... | collective-permute-start | bytes 6291464 | tf_op jit(solution)/shard_map/ppermute | solution.py:11
  30.4 1.3 copy-start.1
  30.4 47.0 %collective-permute-start.1 = (f32[4096,128]{1,0:T(8,128)S(1)}, f32[4096,128]{1,0:T(8,128)}, u32[]{:S(2)}, u32[]{:S(2)}) collective-permute-start(f32[4096,128]{1,0:T(8,128)S(1)} %add_select_fusion.7), channel_id=1, source_target_pairs={{0,2},{1,3},{2,0},{3,1},{4,6},{5,7},{6,4},{7,5},{8,10},{9,11},{10,... | collective-permute-start | bytes 6291464 | tf_op jit(solution)/shard_map/ppermute | solution.py:11
  79.9 47.7 %collective-permute-start.2 = (f32[4096,128]{1,0:T(8,128)S(1)}, f32[4096,128]{1,0:T(8,128)}, u32[]{:S(2)}, u32[]{:S(2)}) collective-permute-start(f32[4096,128]{1,0:T(8,128)S(1)} %add_select_fusion.6), channel_id=1, source_target_pairs={{0,4},{1,5},{2,6},{3,7},{4,0},{5,1},{6,2},{7,3},{8,12},{9,13},{10,... | collective-permute-start | bytes 6291464 | tf_op jit(solution)/shard_map/ppermute | solution.py:11
  130.7 45.4 %collective-permute-start.3 = (f32[4096,128]{1,0:T(8,128)}, f32[4096,128]{1,0:T(8,128)}, u32[]{:S(2)}, u32[]{:S(2)}) collective-permute-start(f32[4096,128]{1,0:T(8,128)} %add_select_fusion.5), channel_id=1, source_target_pairs={{0,8},{1,9},{2,10},{3,11},{4,12},{5,13},{6,14},{7,15},{8,0},{9,1},... | collective-permute-start | bytes 6291464 | tf_op jit(solution)/shard_map/ppermute | solution.py:11
  178.5 45.9 %collective-permute-start.4 = (f32[4096,128]{1,0:T(8,128)S(1)}, f32[4096,128]{1,0:T(8,128)}, u32[]{:S(2)}, u32[]{:S(2)}) collective-permute-start(f32[4096,128]{1,0:T(8,128)S(1)} %add_select_fusion.4), channel_id=1, source_target_pairs={{0,16},{1,17},{2,18},{3,19},{4,20},{5,21},{6,22},{7,23},{8,24},{9,... | collective-permute-start | bytes 6291464 | tf_op jit(solution)/shard_map/ppermute | solution.py:11
  227.6 43.7 %collective-permute-start.5 = (f32[4096,128]{1,0:T(8,128)}, f32[4096,128]{1,0:T(8,128)}, u32[]{:S(2)}, u32[]{:S(2)}) collective-permute-start(f32[4096,128]{1,0:T(8,128)} %add_select_fusion.3), channel_id=1, source_target_pairs={{0,32},{1,33},{2,34},{3,35},{4,36},{5,37},{6,38},{7,39},{8,40},{9,... | collective-permute-start | bytes 6291464 | tf_op jit(solution)/shard_map/ppermute | solution.py:11
  273.8 1.7 copy-start
  273.8 93.3 %collective-permute-start.6 = (f32[4096,128]{1,0:T(8,128)S(1)}, f32[4096,128]{1,0:T(8,128)}, u32[]{:S(2)}, u32[]{:S(2)}) collective-permute-start(f32[4096,128]{1,0:T(8,128)S(1)} %add_select_fusion.2), channel_id=1, source_target_pairs={{0,64},{1,65},{2,66},{3,67},{4,68},{5,69},{6,70},{7,71},{8,72},{9,... | collective-permute-start | bytes 6291464 | tf_op jit(solution)/shard_map/ppermute | solution.py:11
  275.5 99.2 %copy-start.4 = (s32[64]{0:T(128)S(1)}, s32[64]{0:T(128)}, u32[]{:S(2)}) copy-start(s32[64]{0:T(128)} %param.5) | copy-start | bytes 772
  369.5 95.8 %collective-permute-start.7 = (f32[4096,128]{1,0:T(8,128)S(1)}, f32[4096,128]{1,0:T(8,128)}, u32[]{:S(2)}, u32[]{:S(2)}) collective-permute-start(f32[4096,128]{1,0:T(8,128)S(1)} %add_select_fusion.1), channel_id=1, source_target_pairs={{0,128},{1,129},{2,130},{3,131},{4,132},{5,133},{6,134},{7,135},{8... | collective-permute-start | bytes 6291464 | tf_op jit(solution)/shard_map/ppermute | solution.py:11
  470.7 133.0 %copy-start.3 = (f32[64,128]{1,0:T(8,128)}, f32[64,128]{1,0:T(8,128)S(1)}, u32[]{:S(2)}) copy-start(f32[64,128]{1,0:T(8,128)S(1)} %select_multiply_fusion) | copy-start | bytes 98308
Sparse Core Ops, SparseCore 0:
  471.8 125.2 all-gather.2
